TPU v7x, 256 devices: a whole 4x4x8 slice. The times are simulated.
256 devices in a mesh: row: 16 (over y_hi, x, core), col: 16 (over y_lo, z).
Axes of the slice: x: 4, y: 4 (y_hi: 2, y_lo: 2; y = y_hi * 2 + y_lo), z: 8, core: 2. Of those that a mesh axis runs over, the one named last changes fastest.
Arguments:
- amplitudes: bfloat16 [1600, 40960], P('row', 'col'), may hold values from -6 to 6
- integrals: bfloat16 [32768, 40960], P('row', 'col'), may hold values from -0.0390625 to 0.0390625
- row_offsets: int32 [17], replicated, may hold values from 0 to 20438, as said below
- panel_owner: int32 [3], replicated, may hold values from 0 to 15
Outputs:
- residual: float32 [3, 100, 32768], P(None, None, ('row', 'col'))
Inputs may be any that keep to these rules, and one draw needn't show every extreme that they name: row_offsets[0] is 0 and they rise; row block q holds row_offsets[q + 1] - row_offsets[q] live rows, from 512 to 2048, in its first slots; block 0 holds exactly 2048.
All inputs are finite; a program needn't handle non-finite values.
Results may differ from a plain program's by a relative error of at most 0.0003.
Values may be sent and summed in bfloat16 or wider, within the bound.
No kernel may reach another device: no remote copies, remote signals or barrier semaphores. Data moves between devices by JAX's collectives and lax.ppermute only.
A program may use at most 64 MiB of HBM per device.

v0:
```python
import jax
import jax.numpy as jnp
from jax import lax
from jax.sharding import PartitionSpec as P

STEPS = 3


def from_root(block, axis, source):
    block = jnp.where(lax.axis_index(axis) == source, block, jnp.zeros_like(block))
    return lax.psum(block, axis)


def full_product(amp_panel, integrals):
    return lax.dot_general(
        amp_panel, integrals, (((1,), (1,)), ((), ())), preferred_element_type=jnp.float32
    )


def per_device(amplitudes, integrals, row_offsets, panel_owner):
    own_row = lax.axis_index("row")
    live_rows = row_offsets[own_row + 1] - row_offsets[own_row]
    slot_count = integrals.shape[0]
    live_mask = (jnp.arange(slot_count, dtype=jnp.int32) < live_rows).astype(jnp.float32)
    collected = []
    for step in range(STEPS):
        amp_panel = from_root(amplitudes, "row", panel_owner[step])
        product = full_product(amp_panel, integrals)
        term = product * live_mask[None, :]
        collected.append(lax.psum_scatter(term, "col", scatter_dimension=1, tiled=True))
    return jnp.stack(collected)


def solution(mesh):
    return jax.shard_map(
        per_device,
        mesh=mesh,
        in_specs=(P("row", "col"), P("row", "col"), P(), P()),
        out_specs=P(None, None, ("row", "col")),
        check_vma=False,
    )
```

profile of v0, /device:TPU:2, one launch (start us, length us, event | category | flops | bytes accessed | tf_op | source)
XLA Modules:
  0.0 390.7 jit_solution(16907724380133175974)
XLA Ops:
  6.5 0.0 all-reduce.3.cloned.1.call-start
  6.5 1.4 fusion.2
  9.9 2.3 broadcast_select_fusion.2
  12.1 0.0 all-reduce.3.cloned.1.call-update
  12.1 0.0 reduce-scatter.4.cloned.1.call-start
  12.2 1.3 fusion.1
  14.7 143.7 %all-reduce.3.cloned.1.call-done = (bf16[100,2560]{1,0:T(8,128)(2,1)}, bf16[100,2560]{1,0:T(8,128)(2,1)}, bf16[100,2560]{1,0:T(8,128)(2,1)}) async-done(((bf16[100,2560]{1,0:T(8,128)(2,1)}, bf16[100,2560]{1,0:T(8,128)(2,1)}, bf16[100,2560]{1,0:T(8,128)(2,1)}), (bf16[100,2560]{1,0:T(8,128)(2,1)}, bf16[100,2560]{1,0:T(8,128)(2,1)}, bf16[100,2560]{1,0:T(8,128)(2,1)})) %all-reduce.3.cloned.1.call-update) | async-done | bytes 1536016 | tf_op jit(solution)/shard_map/psum | solution.py:11
  158.5 0.0 copy-start.1
  158.5 0.0 copy-start
  158.5 8.5 %convolution_multiply_fusion.2 = f32[100,2048]{1,0:T(8,128)} fusion(bf16[100,2560]{1,0:T(8,128)(2,1)} %get-tuple-element.7, bf16[2048,2560]{1,0:T(8,128)(2,1)} %param.5, f32[2048]{0:T(1024)S(1)} %fusion), kind=kOutput, calls=%fused_computation.2 | convolution fusion | flops 1048780800 | bytes 11825152 | tf_op jit(solution)/shard_map/dot_general | solution.py:15
  166.9 0.0 reduce-scatter.4.cloned.1.call-update
  167.0 0.0 reduce-scatter.6.cloned.1.call-start
  167.0 0.0 copy-done.1
  167.0 8.2 %convolution_multiply_fusion.1 = f32[100,2048]{1,0:T(8,128)} fusion(bf16[100,2560]{1,0:T(8,128)(2,1)S(1)} %copy-done.1, bf16[2048,2560]{1,0:T(8,128)(2,1)} %param.5, f32[2048]{0:T(1024)S(1)} %fusion), kind=kOutput, calls=%fused_computation.1 | convolution fusion | flops 1048780800 | bytes 11825152 | tf_op jit(solution)/shard_map/dot_general | solution.py:15
  175.2 0.0 reduce-scatter.6.cloned.1.call-update
  175.2 0.0 reduce-scatter.8.cloned.1.call-start
  175.3 0.0 copy-done
  175.3 8.2 %convolution_multiply_fusion = f32[100,2048]{1,0:T(8,128)} fusion(bf16[100,2560]{1,0:T(8,128)(2,1)S(1)} %copy-done, bf16[2048,2560]{1,0:T(8,128)(2,1)} %param.5, f32[2048]{0:T(1024)S(1)} %fusion), kind=kOutput, calls=%fused_computation | convolution fusion | flops 1048780800 | bytes 11825152 | tf_op jit(solution)/shard_map/dot_general | solution.py:15
  183.5 0.0 reduce-scatter.8.cloned.1.call-update
  183.5 59.3 %reduce-scatter.4.cloned.1.call-done = f32[100,128]{1,0:T(8,128)} async-done(((f32[100,2048]{1,0:T(8,128)}), f32[100,128]{1,0:T(8,128)}) %reduce-scatter.4.cloned.1.call-update) | async-done | bytes 51216 | tf_op jit(solution)/shard_map/reduce_scatter | solution.py:30
  242.8 69.9 %reduce-scatter.6.cloned.1.call-done = f32[100,128]{1,0:T(8,128)} async-done(((f32[100,2048]{1,0:T(8,128)}), f32[100,128]{1,0:T(8,128)}) %reduce-scatter.6.cloned.1.call-update) | async-done | bytes 51216 | tf_op jit(solution)/shard_map/reduce_scatter | solution.py:30
  312.7 69.9 %reduce-scatter.8.cloned.1.call-done = f32[100,128]{1,0:T(8,128)} async-done(((f32[100,2048]{1,0:T(8,128)}), f32[100,128]{1,0:T(8,128)}) %reduce-scatter.8.cloned.1.call-update) | async-done | bytes 51216 | tf_op jit(solution)/shard_map/reduce_scatter | solution.py:30
  382.6 1.5 pad_maximum_fusion
  (1 shorter events, 0.0 us)
Async XLA Ops:
  6.5 151.9 %all-reduce.3.cloned.1.call-start = ((), (), s32[]{:S(2)}) async-start(), calls=%async_computation.6 | async-start | bytes 3194880 | tf_op jit(solution)/shard_map/psum | solution.py:11
  12.1 230.6 %reduce-scatter.4.cloned.1.call-start = ((), (), s32[]{:S(2)}) async-start(), calls=%async_computation.3 | async-start | bytes 905216 | tf_op jit(solution)/shard_map/reduce_scatter | solution.py:30
  158.5 8.5 %copy-start.1 = (bf16[100,2560]{1,0:T(8,128)(2,1)S(1)}, bf16[100,2560]{1,0:T(8,128)(2,1)}, u32[]{:S(2)}) copy-start(bf16[100,2560]{1,0:T(8,128)(2,1)} %get-tuple-element.6) | copy-start | bytes 1536004
  158.5 16.8 %copy-start = (bf16[100,2560]{1,0:T(8,128)(2,1)S(1)}, bf16[100,2560]{1,0:T(8,128)(2,1)}, u32[]{:S(2)}) copy-start(bf16[100,2560]{1,0:T(8,128)(2,1)} %get-tuple-element.5) | copy-start | bytes 1536004
  167.0 145.7 %reduce-scatter.6.cloned.1.call-start = ((), (), s32[]{:S(2)}) async-start(), calls=%async_computation.4 | async-start | bytes 905216 | tf_op jit(solution)/shard_map/reduce_scatter | solution.py:30
  175.2 207.4 %reduce-scatter.8.cloned.1.call-start = ((), (), s32[]{:S(2)}) async-start(), calls=%async_computation.5 | async-start | bytes 905216 | tf_op jit(solution)/shard_map/reduce_scatter | solution.py:30
Sparse Core Ops, SparseCore 0:
  12.3 146.1 all-reduce.2
  167.1 75.6 reduce-scatter.3
  245.3 67.3 reduce-scatter.5
  315.2 67.3 reduce-scatter.7
where the time goes:
time: 391 us
  waiting for transfers between devices  343 us (88%)
  matrix products  24.8 us (6%)
  between operations  16.3 us (4%)
    reduce_scatter x3, waiting for transfers between devices, per_device(): lax.psum_scatter(term, 'col', scatter_dimension=1, tiled=True)  199 us
    psum x1, waiting for transfers between devices, from_root(): return lax.psum(block, axis)  144 us
    dot_general x3, matrix products, full_product(): lax.dot_general(amp_panel, integrals, (((1,), (1,)), ((), ())), preferred...  24.8 us
  transfers between devices with their start and end apart: 4, of which 4 were waited for; matrix products, arithmetic and copies ran while one was open for 5% of the time, Pallas kernels for 0%

commit v1 on v0

--- a/solution.py
+++ b/solution.py
@@ -8,7 +8,7 @@
 
 def from_root(block, axis, source):
     block = jnp.where(lax.axis_index(axis) == source, block, jnp.zeros_like(block))
-    return lax.psum(block, axis)
+    return jnp.sum(lax.all_gather(block, axis), axis=0)
 
 
 def full_product(amp_panel, integrals):

time: 391 us -> 472 us (1.21)
  waiting for transfers between devices: 343 us -> 408 us
  other arithmetic: 3.8 us -> 18.6 us
    all_gather x0 -> x3, waiting for transfers between devices: none -> 208 us  [from_root(): return jnp.sum(lax.all_gather(block, axis), axis=0)]
    psum x1 -> x0, waiting for transfers between devices: 144 us -> none  [from_root(): return lax.psum(block, axis)]
    reduce_sum x0 -> x3, other arithmetic: none -> 14.8 us  [from_root(): return jnp.sum(lax.all_gather(block, axis), axis=0)]
  transfers between devices with their start and end apart: 4 -> 6, of which waited for: 4 -> 6; matrix products, arithmetic and copies ran while one was open for 5% -> 9% of each run, Pallas kernels for 0% -> 0%
where the time goes in v1:
time: 472 us; the launch traced here: 471 us
  waiting for transfers between devices  408 us (86%)
  matrix products  24.5 us (5%)
  other arithmetic  18.6 us (4%)
  between operations  16.7 us (4%)
    all_gather x3, waiting for transfers between devices, from_root(): return jnp.sum(lax.all_gather(block, axis), axis=0)  208 us
    reduce_scatter x3, waiting for transfers between devices, per_device(): lax.psum_scatter(term, 'col', scatter_dimension=1, tiled=True)  199 us
    dot_general x3, matrix products, full_product(): lax.dot_general(amp_panel, integrals, (((1,), (1,)), ((), ())), preferred...  24.5 us
    reduce_sum x3, other arithmetic, from_root(): return jnp.sum(lax.all_gather(block, axis), axis=0)  14.8 us
  transfers between devices with their start and end apart: 6, of which 6 were waited for; matrix products, arithmetic and copies ran while one was open for 9% of the time, Pallas kernels for 0%

profile of v1, /device:TPU:2, one launch (start us, length us, event | category | flops | bytes accessed | tf_op | source)
XLA Modules:
  0.0 471.1 jit_solution(7438642600142711256)
XLA Ops:
  6.5 0.0 all-gather.14.cloned.1.call-start
  6.5 1.4 fusion.1
  9.8 2.3 select_bitcast_fusion.2
  12.1 0.0 all-gather.14.cloned.1.call-update
  12.1 0.0 all-gather.12.cloned.1.call-start
  12.2 0.7 all-gather.12.cloned.1.call-update
  12.9 0.0 all-gather.10.cloned.1.call-start
  12.9 0.7 all-gather.10.cloned.1.call-update
  13.6 0.0 reduce-scatter.8.cloned.1.call-start
  13.7 1.4 fusion.2
  16.3 76.1 %all-gather.14.cloned.1.call-done = bf16[16,100,2560]{2,1,0:T(8,128)(2,1)} async-done(((bf16[1,100,2560]{2,1,0:T(8,128)(2,1)}), bf16[16,100,2560]{2,1,0:T(8,128)(2,1)}) %all-gather.14.cloned.1.call-update) | async-done | bytes 8192016 | tf_op jit(solution)/shard_map/all_gather | solution.py:11
  92.4 4.9 %reduce_sum.38 = bf16[100,2560]{1,0:T(8,128)(2,1)S(1)} reduce(bf16[16,100,2560]{2,1,0:T(8,128)(2,1)} %all-gather.14.cloned.1.call-done, bf16[]{:T(256)} %constant.14.clone.1), dimensions={0}, to_apply=%region_4.5 | reduce | flops 3840000 | bytes 8704002 | tf_op jit(solution)/shard_map/reduce_sum | solution.py:11
  97.3 8.2 %convolution_multiply_fusion = f32[100,2048]{1,0:T(8,128)} fusion(bf16[100,2560]{1,0:T(8,128)(2,1)S(1)} %reduce_sum.38, bf16[2048,2560]{1,0:T(8,128)(2,1)} %param.5, f32[2048]{0:T(1024)S(1)} %fusion), kind=kOutput, calls=%fused_computation | convolution fusion | flops 1048780800 | bytes 11825152 | tf_op jit(solution)/shard_map/dot_general | solution.py:15
  105.5 0.0 reduce-scatter.8.cloned.1.call-update
  105.5 0.0 reduce-scatter.6.cloned.1.call-start
  105.5 65.9 %all-gather.12.cloned.1.call-done = bf16[16,100,2560]{2,1,0:T(8,128)(2,1)} async-done(((bf16[1,100,2560]{2,1,0:T(8,128)(2,1)}), bf16[16,100,2560]{2,1,0:T(8,128)(2,1)}) %all-gather.12.cloned.1.call-update) | async-done | bytes 8192016 | tf_op jit(solution)/shard_map/all_gather | solution.py:11
  171.4 4.9 %reduce_sum.37 = bf16[100,2560]{1,0:T(8,128)(2,1)S(1)} reduce(bf16[16,100,2560]{2,1,0:T(8,128)(2,1)} %all-gather.12.cloned.1.call-done, bf16[]{:T(256)} %constant.14.clone.1), dimensions={0}, to_apply=%region_2.3 | reduce | flops 3840000 | bytes 8704002 | tf_op jit(solution)/shard_map/reduce_sum | solution.py:11
  176.3 8.2 %convolution_multiply_fusion.1 = f32[100,2048]{1,0:T(8,128)} fusion(bf16[100,2560]{1,0:T(8,128)(2,1)S(1)} %reduce_sum.37, bf16[2048,2560]{1,0:T(8,128)(2,1)} %param.5, f32[2048]{0:T(1024)S(1)} %fusion), kind=kOutput, calls=%fused_computation.1 | convolution fusion | flops 1048780800 | bytes 11825152 | tf_op jit(solution)/shard_map/dot_general | solution.py:15
  184.6 0.0 reduce-scatter.6.cloned.1.call-update
  184.6 0.0 reduce-scatter.4.cloned.1.call-start
  184.7 65.8 %all-gather.10.cloned.1.call-done = bf16[16,100,2560]{2,1,0:T(8,128)(2,1)} async-done(((bf16[1,100,2560]{2,1,0:T(8,128)(2,1)}), bf16[16,100,2560]{2,1,0:T(8,128)(2,1)}) %all-gather.10.cloned.1.call-update) | async-done | bytes 8192016 | tf_op jit(solution)/shard_map/all_gather | solution.py:11
  250.4 4.9 %reduce_sum.36 = bf16[100,2560]{1,0:T(8,128)(2,1)S(1)} reduce(bf16[16,100,2560]{2,1,0:T(8,128)(2,1)} %all-gather.10.cloned.1.call-done, bf16[]{:T(256)} %constant.14.clone.1), dimensions={0}, to_apply=%region_0.1 | reduce | flops 3840000 | bytes 8704002 | tf_op jit(solution)/shard_map/reduce_sum | solution.py:11
  255.4 8.2 %convolution_multiply_fusion.2 = f32[100,2048]{1,0:T(8,128)} fusion(bf16[100,2560]{1,0:T(8,128)(2,1)S(1)} %reduce_sum.36, bf16[2048,2560]{1,0:T(8,128)(2,1)} %param.5, f32[2048]{0:T(1024)S(1)} %fusion), kind=kOutput, calls=%fused_computation.2 | convolution fusion | flops 1048780800 | bytes 11825152 | tf_op jit(solution)/shard_map/dot_general | solution.py:15
  263.5 0.0 reduce-scatter.4.cloned.1.call-update
  263.5 59.7 %reduce-scatter.8.cloned.1.call-done = f32[100,128]{1,0:T(8,128)} async-done(((f32[100,2048]{1,0:T(8,128)}), f32[100,128]{1,0:T(8,128)}) %reduce-scatter.8.cloned.1.call-update) | async-done | bytes 51216 | tf_op jit(solution)/shard_map/reduce_scatter | solution.py:30
  323.2 69.8 %reduce-scatter.6.cloned.1.call-done = f32[100,128]{1,0:T(8,128)} async-done(((f32[100,2048]{1,0:T(8,128)}), f32[100,128]{1,0:T(8,128)}) %reduce-scatter.6.cloned.1.call-update) | async-done | bytes 51216 | tf_op jit(solution)/shard_map/reduce_scatter | solution.py:30
  393.0 69.7 %reduce-scatter.4.cloned.1.call-done = f32[100,128]{1,0:T(8,128)} async-done(((f32[100,2048]{1,0:T(8,128)}), f32[100,128]{1,0:T(8,128)}) %reduce-scatter.4.cloned.1.call-update) | async-done | bytes 51216 | tf_op jit(solution)/shard_map/reduce_scatter | solution.py:30
  462.7 1.5 pad_maximum_fusion
  (1 shorter events, 0.0 us)
Async XLA Ops:
  6.5 85.8 %all-gather.14.cloned.1.call-start = ((), (), s32[]{:S(2)}) async-start(), calls=%async_computation.8 | async-start | bytes 9052160 | tf_op jit(solution)/shard_map/all_gather | solution.py:11
  12.1 159.3 %all-gather.12.cloned.1.call-start = ((), (), s32[]{:S(2)}) async-start(), calls=%async_computation.7 | async-start | bytes 9052160 | tf_op jit(solution)/shard_map/all_gather | solution.py:11
  12.9 237.6 %all-gather.10.cloned.1.call-start = ((), (), s32[]{:S(2)}) async-start(), calls=%async_computation.6 | async-start | bytes 9052160 | tf_op jit(solution)/shard_map/all_gather | solution.py:11
  13.6 309.6 %reduce-scatter.8.cloned.1.call-start = ((), (), s32[]{:S(2)}) async-start(), calls=%async_computation.5 | async-start | bytes 905216 | tf_op jit(solution)/shard_map/reduce_scatter | solution.py:30
  105.5 287.5 %reduce-scatter.6.cloned.1.call-start = ((), (), s32[]{:S(2)}) async-start(), calls=%async_computation.4 | async-start | bytes 905216 | tf_op jit(solution)/shard_map/reduce_scatter | solution.py:30
  184.6 278.1 %reduce-scatter.4.cloned.1.call-start = ((), (), s32[]{:S(2)}) async-start(), calls=%async_computation.3 | async-start | bytes 905216 | tf_op jit(solution)/shard_map/reduce_scatter | solution.py:30
Sparse Core Ops, SparseCore 0:
  12.3 80.0 all-gather.13
  95.1 76.2 all-gather.11
  174.1 76.2 all-gather.9
  252.8 70.3 reduce-scatter.7
  325.8 67.2 reduce-scatter.5
  395.4 67.3 reduce-scatter.3
